TPU v7x, 128 devices: a whole 4x4x4 slice. The times are simulated.
128 devices in a mesh: rep: 4 (over z_lo, core), shard: 32 (over z_hi, x, y).
Axes of the slice: x: 4, y: 4, z: 4 (z_hi: 2, z_lo: 2; z = z_hi * 2 + z_lo), core: 2. Of those that a mesh axis runs over, the one named last changes fastest.
Arguments:
- local_layers: float32 [4, 4, 768, 768], P('rep', None, 'shard'), may hold values from -6 to 6
- global_layers: float32 [4, 768, 768], P(None, 'shard'), may hold values from -6 to 6
- momentum_layers: float32 [4, 768, 768], P(None, 'shard'), may hold values from -3 to 3
- local_embed: float32 [4, 32128, 768], P('rep', 'shard'), may hold values from -6 to 6
- global_embed: float32 [32128, 768], P('shard'), may hold values from -6 to 6
- momentum_embed: float32 [32128, 768], P('shard'), may hold values from -3 to 3
- proj_basis: float32 [768, 64], replicated, may hold values from -0.21875 to 0.21875
Outputs:
- mean_layers: float32 [4, 768, 768], P(None, 'shard')
- moment_layers: float32 [4, 768, 768], P(None, 'shard')
- weights_layers: float32 [4, 768, 768], P(None, 'shard')
- copy_layers: bfloat16 [4, 768, 768], replicated
- mean_embed: float32 [32128, 768], P('shard')
- moment_embed: float32 [32128, 768], P('shard')
- weights_embed: float32 [32128, 768], P('shard')
All inputs are finite; a program needn't handle non-finite values.
Results may differ from a plain program's by a relative error of at most 0.0085.
Values may be sent and summed in bfloat16 or wider, within the bound.
A program may use at most 128 MiB of HBM per device.

v0:
```python
import jax
import jax.numpy as jnp
from jax import lax
from jax.sharding import PartitionSpec as P

OUTER_MOMENTUM = 0.9
OUTER_RATE = 0.7


def outer_update(mean_diff, momentum, weights):
    new_moment = OUTER_MOMENTUM * momentum + mean_diff
    new_weights = weights - OUTER_RATE * (mean_diff + OUTER_MOMENTUM * new_moment)
    return (new_moment, new_weights)


def body(
    local_layers,
    global_layers,
    momentum_layers,
    local_embed,
    global_embed,
    momentum_embed,
    proj_basis,
):
    groups = lax.axis_size("rep")
    layer_diff = global_layers - local_layers[0]
    mean_layers = lax.psum(layer_diff, "rep") / groups
    moment_layers, weights_layers = outer_update(mean_layers, momentum_layers, global_layers)
    copy_layers = lax.all_gather(weights_layers.astype(jnp.bfloat16), "shard", axis=1, tiled=True)
    embed_diff = global_embed - local_embed[0]
    embed_full = lax.psum(embed_diff.astype(jnp.bfloat16), "rep").astype(jnp.float32) / groups
    low_mean = jnp.dot(embed_full, proj_basis, precision=lax.Precision.HIGHEST)
    mean_embed = jnp.dot(low_mean, proj_basis.T, precision=lax.Precision.HIGHEST)
    moment_embed, weights_embed = outer_update(mean_embed, momentum_embed, global_embed)
    return (
        mean_layers,
        moment_layers,
        weights_layers,
        copy_layers,
        mean_embed,
        moment_embed,
        weights_embed,
    )


def solution(mesh):
    in_specs = (
        P("rep", None, "shard", None),
        P(None, "shard", None),
        P(None, "shard", None),
        P("rep", "shard", None),
        P("shard", None),
        P("shard", None),
        P(),
    )
    out_specs = (
        P(None, "shard", None),
        P(None, "shard", None),
        P(None, "shard", None),
        P(),
        P("shard", None),
        P("shard", None),
        P("shard", None),
    )
    return jax.shard_map(body, mesh=mesh, in_specs=in_specs, out_specs=out_specs, check_vma=False)
```

profile of v0, /device:TPU:0, one launch (start us, length us, event | category | flops | bytes accessed | tf_op | source)
XLA Modules:
  0.0 204.0 jit_solution(15389995576287154729)
XLA Ops:
  7.2 0.0 copy-start
  7.2 0.0 all-reduce.3.cloned.1.call-start
  7.2 1.8 bitcast_subtract_fusion.1
  9.1 0.0 all-reduce.3.cloned.1.call-update
  9.1 0.0 all-reduce.5.cloned.1.call-start
  9.1 4.3 %fusion = bf16[1004,768]{1,0:T(8,128)(2,1)} fusion(f32[1004,768]{1,0:T(8,128)} %param.11, f32[1,1004,768]{2,0,1:T(1,128)} %param.10), kind=kLoop, calls=%fused_computation.1 | loop fusion | flops 1542144 | bytes 7710720 | tf_op jit(solution)/shard_map/convert_element_type | solution.py:31
  13.5 0.0 copy-start.1
  13.5 0.0 all-reduce.5.cloned.1.call-update
  13.5 0.0 all-gather.2.cloned.1.call-start
  13.5 36.6 %all-reduce.3.cloned.1.call-done = f32[4,24,768]{2,1,0:T(8,128)} async-done(((f32[4,24,768]{2,1,0:T(8,128)}), f32[4,24,768]{2,1,0:T(8,128)}) %all-reduce.3.cloned.1.call-update) | async-done | bytes 294928 | tf_op jit(solution)/shard_map/psum | solution.py:27
  50.2 2.2 %fusion.6 = (bf16[4,24,768]{2,1,0:T(8,128)(2,1)}, f32[4,24,768]{2,1,0:T(8,128)}, f32[4,24,768]{2,1,0:T(8,128)}, f32[4,24,768]{2,1,0:T(8,128)}) fusion(f32[4,24,768]{2,1,0:T(8,128)} %param.8, f32[4,24,768]{2,1,0:T(8,128)} %param.9, f32[4,24,768]{2,1,0:T(8,128)} %all-reduce.3.cloned.1.call-done), kind=kLoop, calls=%fused_computation.13 | loop fusion | flops 589824 | bytes 1916928 | tf_op jit(solution)/shard_map/convert_element_type | solution.py:29
  52.3 0.0 all-gather.2.cloned.1.call-update
  52.3 50.6 %all-reduce.5.cloned.1.call-done = bf16[1004,768]{1,0:T(8,128)(2,1)} async-done(((bf16[1004,768]{1,0:T(8,128)(2,1)}), bf16[1004,768]{1,0:T(8,128)(2,1)}) %all-reduce.5.cloned.1.call-update) | async-done | bytes 1542160 | tf_op jit(solution)/shard_map/psum | solution.py:31
  103.0 0.0 copy-done
  103.0 3.9 %fusion.1 = f32[1004,64]{1,0:T(8,128)S(1)} fusion(f32[768,64]{0,1:T(8,128)S(1)} %copy-done, bf16[1004,768]{1,0:T(8,128)(2,1)} %all-reduce.5.cloned.1.call-done), kind=kOutput, calls=%fused_computation.4 | convolution fusion | flops 593725440 | bytes 1995776 | tf_op jit(solution)/shard_map/dot_general | solution.py:32
  106.9 0.0 copy-done.1
  106.9 8.7 %multiply_subtract_fusion = (f32[1004,768]{1,0:T(8,128)}, f32[1004,768]{1,0:T(8,128)}, f32[1004,768]{1,0:T(8,128)}) fusion(f32[1004,768]{1,0:T(8,128)S(1)} %copy-done.1, f32[1004,768]{1,0:T(8,128)} %param.12, f32[1004,64]{1,0:T(8,128)S(1)} %fusion.1, f32[768,64]{0,1:T(8,128)S(1)} %copy-done), kind=kOutput, calls=%fused_computation.2 | convolution fusion | flops 596809728 | bytes 15875072 | tf_op jit(solution)/shard_map/dot_general | solution.py:33
  115.6 77.1 %all-gather.2.cloned.1.call-done = bf16[4,768,768]{2,1,0:T(8,128)(2,1)} async-done(((bf16[4,24,768]{2,1,0:T(8,128)(2,1)}), bf16[4,768,768]{2,1,0:T(8,128)(2,1)}) %all-gather.2.cloned.1.call-update) | async-done | bytes 4718608 | tf_op jit(solution)/shard_map/all_gather | solution.py:29
  192.7 4.8 %copy.19 = bf16[4,768,768]{2,1,0:T(8,128)(2,1)} copy(bf16[4,768,768]{2,1,0:T(8,128)(2,1)} %all-gather.2.cloned.1.call-done) | data formatting | bytes 9437184
Async XLA Ops:
  7.2 95.8 %copy-start = (f32[768,64]{0,1:T(8,128)S(1)}, f32[768,64]{0,1:T(8,128)}, u32[]{:S(2)}) copy-start(f32[768,64]{0,1:T(8,128)} %param.13) | copy-start | bytes 589828
  7.2 43.0 %all-reduce.3.cloned.1.call-start = ((), (), s32[]{:S(2)}) async-start(), calls=%async_computation | async-start | bytes 589824 | tf_op jit(solution)/shard_map/psum | solution.py:27
  9.1 93.9 %all-reduce.5.cloned.1.call-start = ((), (), s32[]{:S(2)}) async-start(), calls=%async_computation.2 | async-start | bytes 3096576 | tf_op jit(solution)/shard_map/psum | solution.py:31
  13.5 93.4 %copy-start.1 = (f32[1004,768]{1,0:T(8,128)S(1)}, f32[1004,768]{1,0:T(8,128)}, u32[]{:S(2)}) copy-start(f32[1004,768]{1,0:T(8,128)} %param.11) | copy-start | bytes 9252868
  13.5 179.2 %all-gather.2.cloned.1.call-start = ((), (), s32[]{:S(2)}) async-start(), calls=%async_computation.1 | async-start | bytes 4866048 | tf_op jit(solution)/shard_map/all_gather | solution.py:29
Sparse Core Ops, SparseCore 0:
  11.1 39.0 all-reduce.2
  53.3 49.6 all-reduce.4
  106.6 86.0 all-gather.1
where the time goes:
time: 204 us
  waiting for transfers between devices  164 us (80%)
  between operations  13.8 us (7%)
  matrix products  12.6 us (6%)
  other arithmetic  8.33 us (4%)
  local copies, waits for them, and re-layouts  4.84 us (2%)
    all_gather x1, waiting for transfers between devices, body(): lax.all_gather(weights_layers.astype(jnp.bfloat16), 'shard', axis=1, tile...  77.1 us
    psum x1, waiting for transfers between devices, body(): lax.psum(embed_diff.astype(jnp.bfloat16), 'rep').astype(jnp.float32)  50.6 us
    psum x1, waiting for transfers between devices, body(): mean_layers = lax.psum(layer_diff, 'rep') / groups  36.6 us
    dot_general x1, matrix products, body(): jnp.dot(low_mean, proj_basis.T, precision=lax.Precision.HIGHEST)  8.67 us
    unnamed x5, local copies, waits for them, and re-layouts  4.84 us
    convert_element_type x1, other arithmetic, body(): embed_diff.astype(jnp.bfloat16)  4.34 us
  transfers between devices with their start and end apart: 3, of which 3 were waited for; matrix products, arithmetic and copies ran while one was open for 9% of the time, Pallas kernels for 0%

commit v1 on v0

--- a/solution.py
+++ b/solution.py
@@ -26,7 +26,12 @@
     layer_diff = global_layers - local_layers[0]
     mean_layers = lax.psum(layer_diff, "rep") / groups
     moment_layers, weights_layers = outer_update(mean_layers, momentum_layers, global_layers)
-    copy_layers = lax.all_gather(weights_layers.astype(jnp.bfloat16), "shard", axis=1, tiled=True)
+    copy_layers = jnp.concatenate(
+        lax.all_to_all(
+            jnp.stack([weights_layers.astype(jnp.bfloat16)] * lax.axis_size("shard")), "shard", 0, 0
+        ),
+        axis=1,
+    )
     embed_diff = global_embed - local_embed[0]
     embed_full = lax.psum(embed_diff.astype(jnp.bfloat16), "rep").astype(jnp.float32) / groups
     low_mean = jnp.dot(embed_full, proj_basis, precision=lax.Precision.HIGHEST)

time: 204 us -> 184 us (0.902)
  waiting for transfers between devices: 164 us -> 130 us
  starting transfers between devices: 0.12 us -> 9.84 us
  local copies, waits for them, and re-layouts: 4.84 us -> 7.58 us
    all_gather x1 -> x0, waiting for transfers between devices: 77.1 us -> none  [body(): lax.all_gather(weights_layers.astype(jnp.bfloat16), 'shard', axis=1, tile...]
    psum x1, waiting for transfers between devices: 50.6 us -> 89.1 us  [body(): lax.psum(embed_diff.astype(jnp.bfloat16), 'rep').astype(jnp.float32)]
    all_to_all x0 -> x1, starting transfers between devices: none -> 9.76 us  [body(): lax.all_to_all(jnp.stack([weights_layers.astype(jnp.bfloat16)] * lax.axis...]
    all_to_all x0 -> x1, local copies, waits for them, and re-layouts: none -> 4.83 us  [body(): lax.all_to_all(jnp.stack([weights_layers.astype(jnp.bfloat16)] * lax.axis...]
    unnamed x5 -> x4, local copies, waits for them, and re-layouts: 4.84 us -> 0.01 us
    psum x1, waiting for transfers between devices: 36.6 us -> 41.1 us  [body(): mean_layers = lax.psum(layer_diff, 'rep') / groups]
    another operation x0 -> x1, local copies, waits for them, and re-layouts: none -> 2.73 us  [body(): jnp.stack([weights_layers.astype(jnp.bfloat16)] * lax.axis_size('shard'))]
  transfers between devices with their start and end apart: 3 -> 3, of which waited for: 3 -> 2; matrix products, arithmetic and copies ran while one was open for 9% -> 9% of each run, Pallas kernels for 0% -> 0%
where the time goes in v1:
time: 184 us; the launch traced here: 182 us
  waiting for transfers between devices  130 us (71%)
  between operations  14.1 us (8%)
  matrix products  13.2 us (7%)
  starting transfers between devices  9.84 us (5%)
  local copies, waits for them, and re-layouts  7.58 us (4%)
  other arithmetic  7.34 us (4%)
    psum x1, waiting for transfers between devices, body(): lax.psum(embed_diff.astype(jnp.bfloat16), 'rep').astype(jnp.float32)  89.1 us
    psum x1, waiting for transfers between devices, body(): mean_layers = lax.psum(layer_diff, 'rep') / groups  41.1 us
    all_to_all x1, starting transfers between devices, body(): lax.all_to_all(jnp.stack([weights_layers.astype(jnp.bfloat16)] * lax.axis...  9.76 us
    dot_general x1, matrix products, body(): jnp.dot(low_mean, proj_basis.T, precision=lax.Precision.HIGHEST)  8.74 us
    all_to_all x1, local copies, waits for them, and re-layouts, body(): lax.all_to_all(jnp.stack([weights_layers.astype(jnp.bfloat16)] * lax.axis...  4.83 us
    dot_general x1, matrix products, body(): low_mean = jnp.dot(embed_full, proj_basis, precision=lax.Precision.HIGHEST)  4.47 us
  transfers between devices with their start and end apart: 3, of which 2 were waited for; matrix products, arithmetic and copies ran while one was open for 9% of the time, Pallas kernels for 0%

profile of v1, /device:TPU:0, one launch (start us, length us, event | category | flops | bytes accessed | tf_op | source)
XLA Modules:
  0.0 182.2 jit_solution(8589102730722269212)
XLA Ops:
  7.2 0.0 copy-start
  7.2 0.0 all-reduce.3.cloned.1.call-start
  7.2 1.8 %bitcast_subtract_fusion.1 = f32[4,24,768]{2,1,0:T(8,128)} fusion(f32[4,24,768]{2,1,0:T(8,128)} %param.8, f32[1,4,24,768]{3,2,1,0:T(8,128)} %param.7), kind=kLoop, calls=%fused_computation.8 | loop fusion | flops 73728 | bytes 884736 | tf_op jit(solution)/shard_map/sub | solution.py:26
  9.1 0.0 all-reduce.3.cloned.1.call-update
  9.1 41.1 %all-reduce.3.cloned.1.call-done = f32[4,24,768]{2,1,0:T(8,128)} async-done(((f32[4,24,768]{2,1,0:T(8,128)}), f32[4,24,768]{2,1,0:T(8,128)}) %all-reduce.3.cloned.1.call-update) | async-done | bytes 294928 | tf_op jit(solution)/shard_map/psum | solution.py:27
  50.2 2.1 %fusion.6 = (bf16[4,24,768]{2,1,0:T(8,128)(2,1)S(1)}, f32[4,24,768]{2,1,0:T(8,128)}, f32[4,24,768]{2,1,0:T(8,128)}, f32[4,24,768]{2,1,0:T(8,128)}) fusion(f32[4,24,768]{2,1,0:T(8,128)} %param.8, f32[4,24,768]{2,1,0:T(8,128)} %param.9, f32[4,24,768]{2,1,0:T(8,128)} %all-reduce.3.cloned.1.call-done), kind=kLoop, calls=%fused_computation.13 | loop fusion | flops 589824 | bytes 1916928 | tf_op jit(solution)/shard_map/convert_element_type | solution.py:31
  52.3 2.7 %stack.2 = bf16[32,4,24,768]{3,2,1,0:T(8,128)(2,1)} broadcast(bf16[4,24,768]{2,1,0:T(8,128)(2,1)S(1)} %get-tuple-element.9), dimensions={1,2,3} | broadcast | bytes 4866048 | tf_op jit(solution)/shard_map/stack | solution.py:31
  55.0 0.0 copy-start.1
  55.0 9.8 %all-to-all-start = ((bf16[32,4,24,768]{3,2,1,0:T(8,128)(2,1)}), bf16[32,4,24,768]{3,2,1,0:T(8,128)(2,1)}, u32[]{:S(2)}, u32[]{:S(2)}) async-start(bf16[32,4,24,768]{3,2,1,0:T(8,128)(2,1)} %stack.2), calls=%async_computation | async-start | bytes 9437184 | tf_op jit(solution)/shard_map/all_to_all | solution.py:30
  64.8 0.0 all-reduce.5.cloned.1.call-start
  64.8 0.0 copy-done.1
  64.8 3.4 %fusion = bf16[1004,768]{1,0:T(8,128)(2,1)} fusion(f32[1004,768]{1,0:T(8,128)S(1)} %copy-done.1, f32[1,1004,768]{2,0,1:T(1,128)} %param.10), kind=kLoop, calls=%fused_computation.1 | loop fusion | flops 1542144 | bytes 7710720 | tf_op jit(solution)/shard_map/convert_element_type | solution.py:36
  68.2 0.0 all-reduce.5.cloned.1.call-update
  68.3 89.1 %all-reduce.5.cloned.1.call-done = bf16[1004,768]{1,0:T(8,128)(2,1)} async-done(((bf16[1004,768]{1,0:T(8,128)(2,1)}), bf16[1004,768]{1,0:T(8,128)(2,1)}) %all-reduce.5.cloned.1.call-update) | async-done | bytes 1542160 | tf_op jit(solution)/shard_map/psum | solution.py:36
  157.3 0.0 copy-done
  157.3 4.5 %fusion.1 = f32[1004,64]{0,1:T(8,128)S(1)} fusion(f32[768,64]{0,1:T(8,128)S(1)} %copy-done, bf16[1004,768]{1,0:T(8,128)(2,1)} %all-reduce.5.cloned.1.call-done), kind=kOutput, calls=%fused_computation.4 | convolution fusion | flops 593725440 | bytes 1995776 | tf_op jit(solution)/shard_map/dot_general | solution.py:37
  161.8 8.7 %multiply_subtract_fusion = (f32[1004,768]{1,0:T(8,128)}, f32[1004,768]{1,0:T(8,128)}, f32[1004,768]{1,0:T(8,128)}) fusion(f32[1004,768]{1,0:T(8,128)S(1)} %copy-done.1, f32[1004,768]{1,0:T(8,128)} %param.12, f32[1004,64]{0,1:T(8,128)S(1)} %fusion.1, f32[768,64]{0,1:T(8,128)S(1)} %copy-done), kind=kOutput, calls=%fused_computation.2 | convolution fusion | flops 596809728 | bytes 15875072 | tf_op jit(solution)/shard_map/dot_general | solution.py:38
  170.5 0.0 all-to-all-done
  170.5 4.8 %copy.14 = bf16[32,4,24,768]{3,2,0,1:T(8,128)(2,1)} copy(bf16[32,4,24,768]{3,2,1,0:T(8,128)(2,1)} %all-to-all-done) | data formatting | bytes 9437184 | tf_op jit(solution)/shard_map/all_to_all | solution.py:30
Async XLA Ops:
  7.2 150.2 %copy-start = (f32[768,64]{0,1:T(8,128)S(1)}, f32[768,64]{0,1:T(8,128)}, u32[]{:S(2)}) copy-start(f32[768,64]{0,1:T(8,128)} %param.13) | copy-start | bytes 589828
  7.2 43.0 %all-reduce.3.cloned.1.call-start = ((), (), s32[]{:S(2)}) async-start(), calls=%async_computation.1 | async-start | bytes 589824 | tf_op jit(solution)/shard_map/psum | solution.py:27
  55.0 9.8 %copy-start.1 = (f32[1004,768]{1,0:T(8,128)S(1)}, f32[1004,768]{1,0:T(8,128)}, u32[]{:S(2)}) copy-start(f32[1004,768]{1,0:T(8,128)} %param.11) | copy-start | bytes 9252868
  55.0 115.5 %all-to-all-start = ((bf16[32,4,24,768]{3,2,1,0:T(8,128)(2,1)}), bf16[32,4,24,768]{3,2,1,0:T(8,128)(2,1)}, u32[]{:S(2)}, u32[]{:S(2)}) async-start(bf16[32,4,24,768]{3,2,1,0:T(8,128)(2,1)} %stack.2), calls=%async_computation | async-start | bytes 9437184 | tf_op jit(solution)/shard_map/all_to_all | solution.py:30
  64.8 92.5 %all-reduce.5.cloned.1.call-start = ((), (), s32[]{:S(2)}) async-start(), calls=%async_computation.2 | async-start | bytes 3096576 | tf_op jit(solution)/shard_map/psum | solution.py:36
Sparse Core Ops, SparseCore 0:
  11.1 39.0 all-reduce.2
  68.7 88.5 all-reduce.4

commit v2 on v0

--- a/solution.py
+++ b/solution.py
@@ -28,7 +28,10 @@
     moment_layers, weights_layers = outer_update(mean_layers, momentum_layers, global_layers)
     copy_layers = lax.all_gather(weights_layers.astype(jnp.bfloat16), "shard", axis=1, tiled=True)
     embed_diff = global_embed - local_embed[0]
-    embed_full = lax.psum(embed_diff.astype(jnp.bfloat16), "rep").astype(jnp.float32) / groups
+    embed_full = (
+        jnp.sum(lax.all_gather(embed_diff.astype(jnp.bfloat16), "rep"), axis=0).astype(jnp.float32)
+        / groups
+    )
     low_mean = jnp.dot(embed_full, proj_basis, precision=lax.Precision.HIGHEST)
     mean_embed = jnp.dot(low_mean, proj_basis.T, precision=lax.Precision.HIGHEST)
     moment_embed, weights_embed = outer_update(mean_embed, momentum_embed, global_embed)

time: 204 us -> 218 us (1.069)
  waiting for transfers between devices: 164 us -> 173 us
  other arithmetic: 8.33 us -> 13.5 us
    all_gather x0 -> x1, waiting for transfers between devices: none -> 63.6 us  [body(): lax.all_gather(embed_diff.astype(jnp.bfloat16), 'rep')]
    psum x1 -> x0, waiting for transfers between devices: 50.6 us -> none  [body(): lax.psum(embed_diff.astype(jnp.bfloat16), 'rep').astype(jnp.float32)]
    reduce_sum x0 -> x1, other arithmetic: none -> 5.31 us  [body(): jnp.sum(lax.all_gather(embed_diff.astype(jnp.bfloat16), 'rep'), axis=0)]
    all_gather x1, waiting for transfers between devices: 77.1 us -> 72.5 us  [body(): lax.all_gather(weights_layers.astype(jnp.bfloat16), 'shard', axis=1, tile...]
    unnamed x0 -> x1, other arithmetic: none -> 4.38 us
    convert_element_type x1 -> x0, other arithmetic: 4.34 us -> none  [body(): embed_diff.astype(jnp.bfloat16)]
    unnamed x5 -> x9, local copies, waits for them, and re-layouts: 4.84 us -> 4.85 us
  transfers between devices with their start and end apart: 3 -> 3, of which waited for: 3 -> 3; matrix products, arithmetic and copies ran while one was open for 9% -> 11% of each run, Pallas kernels for 0% -> 0%
where the time goes in v2:
time: 218 us
  waiting for transfers between devices  173 us (79%)
  between operations  13.8 us (6%)
  other arithmetic  13.5 us (6%)
  matrix products  12.6 us (6%)
  local copies, waits for them, and re-layouts  4.85 us (2%)
    all_gather x1, waiting for transfers between devices, body(): lax.all_gather(weights_layers.astype(jnp.bfloat16), 'shard', axis=1, tile...  72.5 us
    all_gather x1, waiting for transfers between devices, body(): lax.all_gather(embed_diff.astype(jnp.bfloat16), 'rep')  63.6 us
    psum x1, waiting for transfers between devices, body(): mean_layers = lax.psum(layer_diff, 'rep') / groups  36.5 us
    dot_general x1, matrix products, body(): jnp.dot(low_mean, proj_basis.T, precision=lax.Precision.HIGHEST)  8.66 us
    reduce_sum x1, other arithmetic, body(): jnp.sum(lax.all_gather(embed_diff.astype(jnp.bfloat16), 'rep'), axis=0)  5.31 us
    unnamed x9, local copies, waits for them, and re-layouts  4.85 us
    unnamed x1, other arithmetic  4.38 us
  transfers between devices with their start and end apart: 3, of which 3 were waited for; matrix products, arithmetic and copies ran while one was open for 11% of the time, Pallas kernels for 0%

profile of v2, /device:TPU:0, one launch (start us, length us, event | category | flops | bytes accessed | tf_op | source)
XLA Modules:
  0.0 217.6 jit_solution(11624790620430092287)
XLA Ops:
  7.2 0.0 copy-start
  7.2 0.0 all-reduce.2.cloned.1.call-start
  7.2 1.8 bitcast_subtract_fusion.1
  9.1 0.0 all-reduce.2.cloned.1.call-update
  9.1 0.0 copy-start.2
  9.1 0.0 copy-start.3
  9.1 0.0 all-gather.7.cloned.1.call-start
  9.2 4.4 %fusion.4 = bf16[1,1004,768]{2,1,0:T(8,128)(2,1)} fusion(f32[1004,768]{1,0:T(8,128)} %param.11, f32[1,1004,768]{2,0,1:T(1,128)} %param.10), kind=kLoop, calls=%fused_computation.7 | loop fusion | flops 1542144 | bytes 7710720
  13.5 0.0 all-gather.7.cloned.1.call-update
  13.6 0.0 all-gather.5.cloned.1.call-start
  13.6 36.5 %all-reduce.2.cloned.1.call-done = f32[4,24,768]{2,1,0:T(8,128)} async-done(((f32[4,24,768]{2,1,0:T(8,128)}), f32[4,24,768]{2,1,0:T(8,128)}) %all-reduce.2.cloned.1.call-update) | async-done | bytes 294928 | tf_op jit(solution)/shard_map/psum | solution.py:27
  50.2 0.0 copy-done.2
  50.2 0.0 copy-done.3
  50.2 2.0 fusion.7
  52.1 0.0 all-gather.5.cloned.1.call-update
  52.2 0.0 copy-start.1
  52.2 63.6 %all-gather.7.cloned.1.call-done = bf16[4,1004,768]{2,1,0:T(8,128)(2,1)} async-done(((bf16[1,1004,768]{2,1,0:T(8,128)(2,1)}), bf16[4,1004,768]{2,1,0:T(8,128)(2,1)}) %all-gather.7.cloned.1.call-update) | async-done | bytes 6168592 | tf_op jit(solution)/shard_map/all_gather | solution.py:32
  115.8 5.3 %reduce_sum.12 = bf16[1004,768]{1,0:T(8,128)(2,1)} reduce(bf16[4,1004,768]{2,1,0:T(8,128)(2,1)} %all-gather.7.cloned.1.call-done, bf16[]{:T(256)} %constant.3.clone.1), dimensions={0}, to_apply=%region_1.0 | reduce | flops 2313216 | bytes 7710722 | tf_op jit(solution)/shard_map/reduce_sum | solution.py:32
  121.1 0.0 copy-done
  121.1 3.9 %fusion.1 = f32[1004,64]{1,0:T(8,128)S(1)} fusion(f32[768,64]{0,1:T(8,128)S(1)} %copy-done, bf16[1004,768]{1,0:T(8,128)(2,1)} %reduce_sum.12), kind=kOutput, calls=%fused_computation.4 | convolution fusion | flops 593725440 | bytes 1995776 | tf_op jit(solution)/shard_map/dot_general | solution.py:35
  125.0 0.0 copy-done.1
  125.0 8.7 %multiply_subtract_fusion = (f32[1004,768]{1,0:T(8,128)}, f32[1004,768]{1,0:T(8,128)}, f32[1004,768]{1,0:T(8,128)}) fusion(f32[1004,768]{1,0:T(8,128)S(1)} %copy-done.1, f32[1004,768]{1,0:T(8,128)} %param.12, f32[1004,64]{1,0:T(8,128)S(1)} %fusion.1, f32[768,64]{0,1:T(8,128)S(1)} %copy-done), kind=kOutput, calls=%fused_computation.2 | convolution fusion | flops 596809728 | bytes 15875072 | tf_op jit(solution)/shard_map/dot_general | solution.py:36
  133.7 72.5 %all-gather.5.cloned.1.call-done = bf16[4,768,768]{2,1,0:T(8,128)(2,1)} async-done(((bf16[4,24,768]{2,1,0:T(8,128)(2,1)}), bf16[4,768,768]{2,1,0:T(8,128)(2,1)}) %all-gather.5.cloned.1.call-update) | async-done | bytes 4718608 | tf_op jit(solution)/shard_map/all_gather | solution.py:29
  206.2 4.8 %copy.20 = bf16[4,768,768]{2,1,0:T(8,128)(2,1)} copy(bf16[4,768,768]{2,1,0:T(8,128)(2,1)} %all-gather.5.cloned.1.call-done) | data formatting | bytes 9437184
Async XLA Ops:
  7.2 113.9 %copy-start = (f32[768,64]{0,1:T(8,128)S(1)}, f32[768,64]{0,1:T(8,128)}, u32[]{:S(2)}) copy-start(f32[768,64]{0,1:T(8,128)} %param.13) | copy-start | bytes 589828
  7.2 43.0 %all-reduce.2.cloned.1.call-start = ((), (), s32[]{:S(2)}) async-start(), calls=%async_computation | async-start | bytes 589824 | tf_op jit(solution)/shard_map/psum | solution.py:27
  9.1 41.1 %copy-start.2 = (f32[4,24,768]{2,1,0:T(8,128)S(1)}, f32[4,24,768]{2,1,0:T(8,128)}, u32[]{:S(2)}) copy-start(f32[4,24,768]{2,1,0:T(8,128)} %param.8) | copy-start | bytes 884740
  9.1 41.1 %copy-start.3 = (f32[4,24,768]{2,1,0:T(8,128)S(1)}, f32[4,24,768]{2,1,0:T(8,128)}, u32[]{:S(2)}) copy-start(f32[4,24,768]{2,1,0:T(8,128)} %param.9) | copy-start | bytes 884740
  9.1 106.7 %all-gather.7.cloned.1.call-start = ((), (), s32[]{:S(2)}) async-start(), calls=%async_computation.2 | async-start | bytes 7741440 | tf_op jit(solution)/shard_map/all_gather | solution.py:32
  13.6 192.7 %all-gather.5.cloned.1.call-start = ((), (), s32[]{:S(2)}) async-start(), calls=%async_computation.1 | async-start | bytes 4866048 | tf_op jit(solution)/shard_map/all_gather | solution.py:29
  52.2 72.9 %copy-start.1 = (f32[1004,768]{1,0:T(8,128)S(1)}, f32[1004,768]{1,0:T(8,128)}, u32[]{:S(2)}) copy-start(f32[1004,768]{1,0:T(8,128)} %param.11) | copy-start | bytes 9252868
Sparse Core Ops, SparseCore 0:
  11.1 39.0 all-reduce.1
  52.4 63.3 all-gather.6
  119.4 86.7 all-gather.4
